TPU v7x, 1024 devices: a whole 8x8x8 slice. The times are simulated.
1024 devices in a mesh: row: 128 (over x, z, core), col: 8 (over y).
Axes of the slice: x: 8, y: 8, z: 8, core: 2. Of those that a mesh axis runs over, the one named last changes fastest.
Arguments:
- p2_panel: bfloat16 [65536, 3584], P('row'), may hold values from -6 to 6
- density: bfloat16 [65536, 3584], P('row', 'col'), may hold values from -0.09375 to 0.09375
- pattern: int32 [1024, 56], P('row'), may hold values 0 or 1
- x_basis: bfloat16 [65536, 32], P('row'), may hold values from -0.59765625 to 0.59765625
- x_offset: int32 [1024], P('row'), may hold values from 0 to 160
- x_extent: int32 [1024], P('row'), may hold values from 1 to 32
- y_basis: bfloat16 [128, 3584, 32], P('row', 'col'), may hold values from -0.59765625 to 0.59765625
- y_offset: int32 [128, 56], P('row', 'col'), may hold values from 0 to 160
- y_extent: int32 [128, 56], P('row', 'col'), may hold values from 1 to 32
Outputs:
- new_density: bfloat16 [65536, 3584], P('row', 'col')
- grid_density: float32 [16384, 1024], P('row', 'col')
Inputs may be any that keep to these rules, and one draw needn't show every extreme that they name: `pattern`: 1 where a block of the window is stored.
All inputs are finite; a program needn't handle non-finite values.
Results may differ from a plain program's by a relative error of at most 0.0049.
Values may be sent and summed in bfloat16 or wider, within the bound.
A program may use at most 64 MiB of HBM per device.

v0:
```python
import jax
import jax.numpy as jnp
from jax import lax
from jax.sharding import PartitionSpec as P

HD = 3
SX = 128
SY = 128
M = 32


def passed_along(value, axis, steps):
    count = lax.axis_size(axis)
    pairs = [(source, (source + steps) % count) for source in range(count)]
    return lax.ppermute(value, axis, pairs)


def mask_blocks(values, pattern):
    number, win_slots = pattern.shape
    block_size = values.shape[0] // number
    shaped = values.reshape(number, block_size, win_slots, block_size)
    return (shaped * pattern.astype(values.dtype)[:, None, :, None]).reshape(values.shape)


def place(tile_vals, offset, extent, length):
    number = offset.shape[0]
    breadth = tile_vals.shape[1]
    blocks = tile_vals.reshape(number, -1, breadth)
    cell_ids = jnp.arange(length, dtype=jnp.int32)
    step_ids = jnp.arange(breadth, dtype=jnp.int32)
    onehot = (cell_ids[None, None, :] == offset[:, None, None] + step_ids[None, :, None]) & (
        step_ids[None, :, None] < extent[:, None, None]
    )
    spread = jnp.einsum(
        "iat,ite->iae", blocks, onehot.astype(blocks.dtype), preferred_element_type=jnp.float32
    )
    return spread.reshape(-1, length).astype(jnp.bfloat16)


def shards(p2_panel, density, pattern, x_basis, x_offset, x_extent, y_basis, y_offset, y_extent):
    col_count = lax.axis_size("col")
    column = lax.axis_index("col")
    row_blocks, win_slots = pattern.shape
    block_size = x_basis.shape[0] // row_blocks
    per_class = win_slots // col_count
    stride = row_blocks // col_count
    panel_rows = row_blocks * block_size
    square = mask_blocks(p2_panel, pattern)
    own_pattern = lax.dynamic_index_in_dim(
        pattern.reshape(row_blocks, per_class, col_count), column, 2, keepdims=False
    )
    own_tile = mask_blocks(density, own_pattern)

    def contribute(summed, distance, incoming):
        first = row_blocks * (distance + HD) * block_size
        panel_cols = square[:, first : first + panel_rows]
        product = jnp.dot(panel_cols, incoming, preferred_element_type=jnp.float32)
        padding = per_class * block_size - incoming.shape[1]
        if distance > 0:
            product = jnp.pad(product, ((0, 0), (padding, 0)))
        elif distance < 0:
            product = jnp.pad(product, ((0, 0), (0, padding)))
        return summed + product

    summed = contribute(jnp.zeros((panel_rows, per_class * block_size), jnp.float32), 0, own_tile)
    lower_tile = own_tile
    upper_tile = own_tile
    for distance in range(1, HD + 1):
        kept_cols = (per_class - stride * distance) * block_size
        lower_tile = passed_along(lower_tile[:, :kept_cols], "row", -1)
        upper_tile = passed_along(upper_tile[:, stride * block_size :], "row", 1)
        summed = contribute(summed, distance, lower_tile)
        summed = contribute(summed, -distance, upper_tile)
    own_square = lax.dynamic_index_in_dim(
        square.reshape(panel_rows, per_class, col_count, block_size), column, 2, keepdims=False
    )
    own_square = own_square.reshape(panel_rows, per_class * block_size)
    renewed = mask_blocks(3.0 * own_square.astype(jnp.float32) - 2.0 * summed, own_pattern).astype(
        jnp.bfloat16
    )
    y_spread = place(y_basis[0], y_offset[0], y_extent[0], SY + 2 * M)
    half_done = jnp.dot(renewed, y_spread, preferred_element_type=jnp.float32).astype(jnp.bfloat16)
    x_spread = place(x_basis, x_offset, x_extent, SX + 2 * M)
    extended = lax.dot_general(
        x_spread, half_done, (((0,), (0,)), ((), ())), preferred_element_type=jnp.float32
    )
    interior = extended[M : M + SX]
    for shift_by, rim_cells, position in ((-1, extended[:M], SX - M), (1, extended[SX + M :], 0)):
        received = passed_along(rim_cells, "row", shift_by)
        interior = interior + jnp.pad(received, ((position, SX - M - position), (0, 0)))
    grid_out = interior[:, M : M + SY]
    for shift_by, rim_cells, position in (
        (-1, interior[:, :M], SY - M),
        (1, interior[:, SY + M :], 0),
    ):
        received = passed_along(rim_cells, "col", shift_by)
        grid_out = grid_out + jnp.pad(received, ((0, 0), (position, SY - M - position)))
    return (renewed, grid_out)


def solution(mesh):
    placed = (
        P("row", None),
        P("row", "col"),
        P("row", None),
        P("row", None),
        P("row"),
        P("row"),
        P("row", "col", None),
        P("row", "col"),
        P("row", "col"),
    )
    return jax.shard_map(
        shards,
        mesh=mesh,
        in_specs=placed,
        out_specs=(P("row", "col"), P("row", "col")),
        check_vma=False,
    )
```

profile of v0, /device:TPU:8, one launch (start us, length us, event | category | flops | bytes accessed | tf_op | source)
XLA Modules:
  0.0 112.0 jit_solution(9796520441349387732)
XLA Ops:
  2.5 1.1 %mul.69 = bf16[512,448]{0,1:T(8,128)(2,1)S(1)} multiply(bf16[512,448]{0,1:T(8,128)(2,1)} %param.10, bf16[512,448]{0,1:T(8,128)(2,1)S(1)} %mul.68) | non-fusion elementwise | flops 229376 | bytes 1376256 | tf_op jit(solution)/shard_map/mul | solution.py:22
  4.6 1.9 %collective-permute-start.1 = (bf16[512,384]{0,1:T(8,128)(2,1)}, bf16[512,384]{0,1:T(8,128)(2,1)}, u32[]{:S(2)}, u32[]{:S(2)}) collective-permute-start(bf16[512,384]{0,1:T(8,128)(2,1)} %get-tuple-element.3), channel_id=1, source_target_pairs={{0,8},{8,16},{16,24},{24,32},{32,40},{40,48},{48,56},{56,64},{64,7... | collective-permute-start | bytes 1179656 | tf_op jit(solution)/shard_map/ppermute | solution.py:15
  6.5 16.7 %collective-permute-start = (bf16[512,384]{0,1:T(8,128)(2,1)}, bf16[512,384]{0,1:T(8,128)(2,1)}, u32[]{:S(2)}, u32[]{:S(2)}) collective-permute-start(bf16[512,384]{0,1:T(8,128)(2,1)} %get-tuple-element.2), channel_id=1, source_target_pairs={{0,1016},{8,0},{16,8},{24,16},{32,24},{40,32},{48,40},{56,48},{64,... | collective-permute-start | bytes 1179656 | tf_op jit(solution)/shard_map/ppermute | solution.py:15
  24.1 1.0 convolution_convert_fusion.1
  25.3 4.0 %mul.64 = bf16[8,64,56,64]{3,2,1,0:T(8,128)(2,1)} broadcast(bf16[8,56]{1,0:T(8,128)(2,1)S(1)} %convert_element_type.73), dimensions={0,2} | broadcast | bytes 3670912 | tf_op jit(solution)/shard_map/mul | solution.py:22
  29.2 9.9 %mul.65 = bf16[512,3584]{1,0:T(8,128)(2,1)} reshape(bf16[8,64,56,64]{3,2,1,0:T(8,128)(2,1)} %mul.64) | data formatting | bytes 7340032 | tf_op jit(solution)/shard_map/mul | solution.py:22
  39.1 5.9 %copy.22 = bf16[512,3584]{0,1:T(8,128)(2,1)} copy(bf16[512,3584]{1,0:T(8,128)(2,1)} %param.9) | data formatting | bytes 7340032 | tf_op args[0]
  45.1 6.0 %mul.66 = bf16[512,3584]{1,0:T(8,128)(2,1)} multiply(bf16[512,3584]{1,0:T(8,128)(2,1)} %param.9, bf16[512,3584]{1,0:T(8,128)(2,1)} %mul.65) | non-fusion elementwise | flops 1835008 | bytes 11010048 | tf_op jit(solution)/shard_map/mul | solution.py:22
  52.1 1.3 %convert_multiply_fusion = f32[512,7,1,64]{0,3,2,1:T(8,128)S(1)} fusion(bf16[512,7,8,64]{0,3,2,1:T(8,128)(2,1)} %bitcast.43, s32[]{:T(128)S(6)} %select_n.6, bf16[512,7,1]{0,2,1:T(2,128)(2,1)S(1)} %constant_dynamic-slice_fusion), kind=kLoop, calls=%fused_computation.7 | loop fusion | flops 688128 | bytes 1383428 | tf_op jit(solution)/shard_map/mul | solution.py:78
  53.4 1.0 slice.84
  54.4 1.9 %collective-permute-start.3 = (bf16[512,320]{0,1:T(8,128)(2,1)S(1)}, bf16[512,320]{0,1:T(8,128)(2,1)S(1)}, u32[]{:S(2)}, u32[]{:S(2)}) collective-permute-start(bf16[512,320]{0,1:T(8,128)(2,1)S(1)} %slice.84), channel_id=1, source_target_pairs={{0,8},{8,16},{16,24},{24,32},{32,40},{40,48},{48,56},{56,64},{64,7... | collective-permute-start | bytes 983048 | tf_op jit(solution)/shard_map/ppermute | solution.py:15
  57.3 7.0 %collective-permute-start.2 = (bf16[512,320]{0,1:T(8,128)(2,1)S(1)}, bf16[512,320]{0,1:T(8,128)(2,1)S(1)}, u32[]{:S(2)}, u32[]{:S(2)}) collective-permute-start(bf16[512,320]{0,1:T(8,128)(2,1)S(1)} %slice.82), channel_id=1, source_target_pairs={{0,1016},{8,0},{16,8},{24,16},{32,24},{40,32},{48,40},{56,48},{64,... | collective-permute-start | bytes 983048 | tf_op jit(solution)/shard_map/ppermute | solution.py:15
  64.3 1.6 %fusion.11 = f32[512,384]{0,1:T(8,128)S(1)} fusion(bf16[512,384]{0,1:T(8,128)(2,1)} %collective-permute-done.1, bf16[512,3584]{1,0:T(8,128)(2,1)} %mul.66), kind=kOutput, calls=%fused_computation.16 | convolution fusion | flops 201326592 | bytes 1703936 | tf_op jit(solution)/shard_map/dot_general | solution.py:57
  65.9 1.4 %fusion.13 = f32[512,384]{0,1:T(8,128)S(1)} fusion(bf16[512,384]{0,1:T(8,128)(2,1)} %collective-permute-done, bf16[512,3584]{1,0:T(8,128)(2,1)S(1)} %copy-done), kind=kOutput, calls=%fused_computation.18 | convolution fusion | flops 201326592 | bytes 1703936 | tf_op jit(solution)/shard_map/dot_general | solution.py:57
  67.3 1.9 %collective-permute-start.5 = (bf16[512,256]{0,1:T(8,128)(2,1)S(1)}, bf16[512,256]{0,1:T(8,128)(2,1)S(1)}, u32[]{:S(2)}, u32[]{:S(2)}) collective-permute-start(bf16[512,256]{0,1:T(8,128)(2,1)S(1)} %slice.88), channel_id=1, source_target_pairs={{0,8},{8,16},{16,24},{24,32},{32,40},{40,48},{48,56},{56,64},{64,7... | collective-permute-start | bytes 786440 | tf_op jit(solution)/shard_map/ppermute | solution.py:15
  69.3 7.0 %collective-permute-start.4 = (bf16[512,256]{0,1:T(8,128)(2,1)S(1)}, bf16[512,256]{0,1:T(8,128)(2,1)S(1)}, u32[]{:S(2)}, u32[]{:S(2)}) collective-permute-start(bf16[512,256]{0,1:T(8,128)(2,1)S(1)} %slice.86), channel_id=1, source_target_pairs={{0,1016},{8,0},{16,8},{24,16},{32,24},{40,32},{48,40},{56,48},{64,... | collective-permute-start | bytes 786440 | tf_op jit(solution)/shard_map/ppermute | solution.py:15
  77.0 1.3 %collective-permute-done.5 = bf16[512,256]{0,1:T(8,128)(2,1)S(1)} collective-permute-done((bf16[512,256]{0,1:T(8,128)(2,1)S(1)}, bf16[512,256]{0,1:T(8,128)(2,1)S(1)}, u32[]{:S(2)}, u32[]{:S(2)}) %collective-permute-start.5) | collective-permute-done | bytes 262176 | tf_op jit(solution)/shard_map/ppermute | solution.py:15
  78.7 1.5 %collective-permute-done.4 = bf16[512,256]{0,1:T(8,128)(2,1)S(1)} collective-permute-done((bf16[512,256]{0,1:T(8,128)(2,1)S(1)}, bf16[512,256]{0,1:T(8,128)(2,1)S(1)}, u32[]{:S(2)}, u32[]{:S(2)}) %collective-permute-start.4) | collective-permute-done | bytes 262176 | tf_op jit(solution)/shard_map/ppermute | solution.py:15
  81.9 7.1 %collective-permute-start.6 = (f32[32,192]{1,0:T(8,128)S(1)}, f32[32,192]{1,0:T(8,128)S(1)}, u32[]{:S(2)}, u32[]{:S(2)}) collective-permute-start(f32[32,192]{1,0:T(8,128)S(1)} %get-tuple-element.4), channel_id=1, source_target_pairs={{0,1016},{8,0},{16,8},{24,16},{32,24},{40,32},{48,40},{56,48},{64,... | collective-permute-start | bytes 73736 | tf_op jit(solution)/shard_map/ppermute | solution.py:15
  89.1 1.9 %collective-permute-start.7 = (f32[32,192]{1,0:T(8,128)S(1)}, f32[32,192]{1,0:T(8,128)S(1)}, u32[]{:S(2)}, u32[]{:S(2)}) collective-permute-start(f32[32,192]{1,0:T(8,128)S(1)} %get-tuple-element.5), channel_id=1, source_target_pairs={{0,8},{8,16},{16,24},{24,32},{32,40},{40,48},{48,56},{56,64},{64,7... | collective-permute-start | bytes 73736 | tf_op jit(solution)/shard_map/ppermute | solution.py:15
  91.0 6.6 %collective-permute-done.7 = f32[32,192]{1,0:T(8,128)S(1)} collective-permute-done((f32[32,192]{1,0:T(8,128)S(1)}, f32[32,192]{1,0:T(8,128)S(1)}, u32[]{:S(2)}, u32[]{:S(2)}) %collective-permute-start.7) | collective-permute-done | bytes 24608 | tf_op jit(solution)/shard_map/ppermute | solution.py:15
  97.7 6.2 %collective-permute-start.8 = (f32[128,32]{1,0:T(8,128)S(1)}, f32[128,32]{1,0:T(8,128)S(1)}, u32[]{:S(2)}, u32[]{:S(2)}) collective-permute-start(f32[128,32]{1,0:T(8,128)S(1)} %get-tuple-element.6), channel_id=1, source_target_pairs={{0,7},{1,0},{2,1},{3,2},{4,3},{5,4},{6,5},{7,6},{8,15},{9,8},{10,9... | collective-permute-start | bytes 49160 | tf_op jit(solution)/shard_map/ppermute | solution.py:15
  103.9 1.9 %collective-permute-start.9 = (f32[128,32]{1,0:T(8,128)S(1)}, f32[128,32]{1,0:T(8,128)S(1)}, u32[]{:S(2)}, u32[]{:S(2)}) collective-permute-start(f32[128,32]{1,0:T(8,128)S(1)} %get-tuple-element.7), channel_id=1, source_target_pairs={{0,1},{1,2},{2,3},{3,4},{4,5},{5,6},{6,7},{7,0},{8,9},{9,10},{10,1... | collective-permute-start | bytes 49160 | tf_op jit(solution)/shard_map/ppermute | solution.py:15
  105.8 5.4 %collective-permute-done.9 = f32[128,32]{1,0:T(8,128)S(1)} collective-permute-done((f32[128,32]{1,0:T(8,128)S(1)}, f32[128,32]{1,0:T(8,128)S(1)}, u32[]{:S(2)}, u32[]{:S(2)}) %collective-permute-start.9) | collective-permute-done | bytes 16416 | tf_op jit(solution)/shard_map/ppermute | solution.py:15
  (60 shorter events, 9.4 us)
Async XLA Ops:
  0.6 24.5 %copy-start.5 = (s32[8,56]{1,0:T(8,128)S(1)}, s32[8,56]{1,0:T(8,128)}, u32[]{:S(2)}) copy-start(s32[8,56]{1,0:T(8,128)} %param.11) | copy-start | bytes 5380
  0.6 22.6 %copy-start.3 = (bf16[512,32]{0,1:T(8,128)(2,1)S(1)}, bf16[512,32]{0,1:T(8,128)(2,1)}, u32[]{:S(2)}) copy-start(bf16[512,32]{0,1:T(8,128)(2,1)} %param.12) | copy-start | bytes 98308
  0.7 22.7 %copy-start.6 = (s32[8]{0:T(128)S(1)}, s32[8]{0:T(128)}, u32[]{:S(2)}) copy-start(s32[8]{0:T(128)} %param.13) | copy-start | bytes 100
  0.7 22.7 %copy-start.8 = (s32[8]{0:T(128)S(1)}, s32[8]{0:T(128)}, u32[]{:S(2)}) copy-start(s32[8]{0:T(128)} %param.14) | copy-start | bytes 100
  0.7 22.8 %copy-start.4 = (bf16[1,448,32]{1,2,0:T(8,128)(2,1)S(1)}, bf16[1,448,32]{1,2,0:T(8,128)(2,1)}, u32[]{:S(2)}) copy-start(bf16[1,448,32]{1,2,0:T(8,128)(2,1)} %param.15) | copy-start | bytes 86020
  0.7 22.9 %copy-start.7 = (s32[1,7]{1,0:T(1,128)S(1)}, s32[1,7]{1,0:T(1,128)}, u32[]{:S(2)}) copy-start(s32[1,7]{1,0:T(1,128)} %param.16) | copy-start | bytes 88
  0.7 23.0 %copy-start.9 = (s32[1,7]{1,0:T(1,128)S(1)}, s32[1,7]{1,0:T(1,128)}, u32[]{:S(2)}) copy-start(s32[1,7]{1,0:T(1,128)} %param.17) | copy-start | bytes 88
  4.6 48.9 %collective-permute-start.1 = (bf16[512,384]{0,1:T(8,128)(2,1)}, bf16[512,384]{0,1:T(8,128)(2,1)}, u32[]{:S(2)}, u32[]{:S(2)}) collective-permute-start(bf16[512,384]{0,1:T(8,128)(2,1)} %get-tuple-element.3), channel_id=1, source_target_pairs={{0,8},{8,16},{16,24},{24,32},{32,40},{40,48},{48,56},{56,64},{64,7... | collective-permute-start | bytes 1179656 | tf_op jit(solution)/shard_map/ppermute | solution.py:15
  6.5 49.9 %collective-permute-start = (bf16[512,384]{0,1:T(8,128)(2,1)}, bf16[512,384]{0,1:T(8,128)(2,1)}, u32[]{:S(2)}, u32[]{:S(2)}) collective-permute-start(bf16[512,384]{0,1:T(8,128)(2,1)} %get-tuple-element.2), channel_id=1, source_target_pairs={{0,1016},{8,0},{16,8},{24,16},{32,24},{40,32},{48,40},{56,48},{64,... | collective-permute-start | bytes 1179656 | tf_op jit(solution)/shard_map/ppermute | solution.py:15
  52.0 13.8 %copy-start = (bf16[512,3584]{1,0:T(8,128)(2,1)S(1)}, bf16[512,3584]{1,0:T(8,128)(2,1)}, u32[]{:S(2)}) copy-start(bf16[512,3584]{1,0:T(8,128)(2,1)} %mul.66) | copy-start | bytes 11010052
  54.4 12.9 %collective-permute-start.3 = (bf16[512,320]{0,1:T(8,128)(2,1)S(1)}, bf16[512,320]{0,1:T(8,128)(2,1)S(1)}, u32[]{:S(2)}, u32[]{:S(2)}) collective-permute-start(bf16[512,320]{0,1:T(8,128)(2,1)S(1)} %slice.84), channel_id=1, source_target_pairs={{0,8},{8,16},{16,24},{24,32},{32,40},{40,48},{48,56},{56,64},{64,7... | collective-permute-start | bytes 983048 | tf_op jit(solution)/shard_map/ppermute | solution.py:15
  57.3 11.9 %collective-permute-start.2 = (bf16[512,320]{0,1:T(8,128)(2,1)S(1)}, bf16[512,320]{0,1:T(8,128)(2,1)S(1)}, u32[]{:S(2)}, u32[]{:S(2)}) collective-permute-start(bf16[512,320]{0,1:T(8,128)(2,1)S(1)} %slice.82), channel_id=1, source_target_pairs={{0,1016},{8,0},{16,8},{24,16},{32,24},{40,32},{48,40},{56,48},{64,... | collective-permute-start | bytes 983048 | tf_op jit(solution)/shard_map/ppermute | solution.py:15
  67.3 11.0 %collective-permute-start.5 = (bf16[512,256]{0,1:T(8,128)(2,1)S(1)}, bf16[512,256]{0,1:T(8,128)(2,1)S(1)}, u32[]{:S(2)}, u32[]{:S(2)}) collective-permute-start(bf16[512,256]{0,1:T(8,128)(2,1)S(1)} %slice.88), channel_id=1, source_target_pairs={{0,8},{8,16},{16,24},{24,32},{32,40},{40,48},{48,56},{56,64},{64,7... | collective-permute-start | bytes 786440 | tf_op jit(solution)/shard_map/ppermute | solution.py:15
  69.3 10.8 %collective-permute-start.4 = (bf16[512,256]{0,1:T(8,128)(2,1)S(1)}, bf16[512,256]{0,1:T(8,128)(2,1)S(1)}, u32[]{:S(2)}, u32[]{:S(2)}) collective-permute-start(bf16[512,256]{0,1:T(8,128)(2,1)S(1)} %slice.86), channel_id=1, source_target_pairs={{0,1016},{8,0},{16,8},{24,16},{32,24},{40,32},{48,40},{56,48},{64,... | collective-permute-start | bytes 786440 | tf_op jit(solution)/shard_map/ppermute | solution.py:15
  80.5 0.9 copy-start.2
  81.1 30.9 %copy-start.1 = (bf16[512,448]{0,1:T(8,128)(2,1)}, bf16[512,448]{0,1:T(8,128)(2,1)S(1)}, u32[]{:S(2)}) copy-start(bf16[512,448]{0,1:T(8,128)(2,1)S(1)} %fusion.2) | copy-start | bytes 1376260
  81.9 9.1 %collective-permute-start.6 = (f32[32,192]{1,0:T(8,128)S(1)}, f32[32,192]{1,0:T(8,128)S(1)}, u32[]{:S(2)}, u32[]{:S(2)}) collective-permute-start(f32[32,192]{1,0:T(8,128)S(1)} %get-tuple-element.4), channel_id=1, source_target_pairs={{0,1016},{8,0},{16,8},{24,16},{32,24},{40,32},{48,40},{56,48},{64,... | collective-permute-start | bytes 73736 | tf_op jit(solution)/shard_map/ppermute | solution.py:15
  89.1 8.6 %collective-permute-start.7 = (f32[32,192]{1,0:T(8,128)S(1)}, f32[32,192]{1,0:T(8,128)S(1)}, u32[]{:S(2)}, u32[]{:S(2)}) collective-permute-start(f32[32,192]{1,0:T(8,128)S(1)} %get-tuple-element.5), channel_id=1, source_target_pairs={{0,8},{8,16},{16,24},{24,32},{32,40},{40,48},{48,56},{56,64},{64,7... | collective-permute-start | bytes 73736 | tf_op jit(solution)/shard_map/ppermute | solution.py:15
  97.7 8.1 %collective-permute-start.8 = (f32[128,32]{1,0:T(8,128)S(1)}, f32[128,32]{1,0:T(8,128)S(1)}, u32[]{:S(2)}, u32[]{:S(2)}) collective-permute-start(f32[128,32]{1,0:T(8,128)S(1)} %get-tuple-element.6), channel_id=1, source_target_pairs={{0,7},{1,0},{2,1},{3,2},{4,3},{5,4},{6,5},{7,6},{8,15},{9,8},{10,9... | collective-permute-start | bytes 49160 | tf_op jit(solution)/shard_map/ppermute | solution.py:15
  103.9 7.4 %collective-permute-start.9 = (f32[128,32]{1,0:T(8,128)S(1)}, f32[128,32]{1,0:T(8,128)S(1)}, u32[]{:S(2)}, u32[]{:S(2)}) collective-permute-start(f32[128,32]{1,0:T(8,128)S(1)} %get-tuple-element.7), channel_id=1, source_target_pairs={{0,1},{1,2},{2,3},{3,4},{4,5},{5,6},{6,7},{7,0},{8,9},{9,10},{10,1... | collective-permute-start | bytes 49160 | tf_op jit(solution)/shard_map/ppermute | solution.py:15
where the time goes:
time: 113 us; the launch traced here: 112 us
  starting transfers between devices  53.6 us (47%)
  local copies, waits for them, and re-layouts  26.2 us (23%)
  waiting for transfers between devices  14.9 us (13%)
  other arithmetic  9.52 us (8%)
  matrix products  6.87 us (6%)
    ppermute x10, starting transfers between devices, passed_along(): return lax.ppermute(value, axis, pairs)  53.6 us
    mul x8, local copies, waits for them, and re-layouts, mask_blocks(): shaped * pattern.astype(values.dtype)[:, None, :, None]  15.5 us
    ppermute x10, waiting for transfers between devices, passed_along(): return lax.ppermute(value, axis, pairs)  14.9 us
    mul x2, other arithmetic, mask_blocks(): shaped * pattern.astype(values.dtype)[:, None, :, None]  7.09 us
    unnamed x21, local copies, waits for them, and re-layouts  6.2 us
    dot_general x7, matrix products, contribute(): product = jnp.dot(panel_cols, incoming, preferred_element_type=jnp.float32)  4.97 us
  transfers between devices with their start and end apart: 10, of which 4 were waited for; matrix products, arithmetic and copies ran while one was open for 32% of the time, Pallas kernels for 0%

commit v1 on v0

v1 whole, which is shorter than its diff:
```python
import functools

import jax
import jax.numpy as jnp
from jax import lax
from jax.experimental import pallas as pl
from jax.experimental.pallas import tpu as pltpu
from jax.sharding import PartitionSpec as P

MESH = pl.DeviceIdType.MESH
BS = 64
BR = 8
CLASSES = 8
WC = 7
W = 56
PANEL = 512
TILE = 128
CELLS = 192
SX = 128
MARGIN = 32
F32 = jnp.float32
BF16 = jnp.bfloat16

UP = {
    1: ((320, 128), (192, 128), (64, 128)),
    2: ((320, 128), (192, 128), (128, 64)),
    3: ((320, 128), (192, 128)),
}
DOWN = {
    1: ((0, 128), (128, 128), (256, 128)),
    2: ((0, 128), (128, 128), (256, 64)),
    3: ((0, 128), (128, 128)),
}
FIRST = {1: 0, 2: 3, 3: 6}
BASE = {1: 0, 2: 384, 3: 704}
IN_ROWS = 960


def dot_nt(left, right):
    return lax.dot_general(left, right, (((1,), (1,)), ((), ())), preferred_element_type=F32)


def kernel(
    rows, cols,
    p2, dens, pat, xb, xo, xe, yb, yo, ye,
    out_new, out_grid,
    s, dv, pv, xbv, ybv, xov, xev, yov, yev,
    own, up_in, down_in, acc, spread_x, spread_y, mask_rows, ext, packed, halo,
    load_sem, send_sem, up_sem, down_sem, hsend_sem, halo_sem,
):
    r = lax.axis_index("row")
    c = lax.axis_index("col")
    even = lax.rem(r, 2) == 0
    odd = lax.rem(r, 2) == 1

    def at(dr, dc):
        return (lax.rem(r + (dr + rows), rows), lax.rem(c + (dc + cols), cols))

    barrier = pltpu.get_barrier_semaphore()
    friends = [(-1, 0), (1, 0), (-2, 0), (2, 0), (0, -1), (0, 1), (-1, -1), (-1, 1), (1, -1), (1, 1)]
    for dr, dc in friends:
        pl.semaphore_signal(barrier, inc=1, device_id=at(dr, dc), device_id_type=MESH)

    loads = []
    for number, (source, target) in enumerate(
        ((dens, dv), (pat, pv), (xb, xbv), (yb, ybv), (xo, xov), (xe, xev), (yo, yov), (ye, yev))
    ):
        loads.append(pltpu.make_async_copy(source, target, load_sem.at[number]))
    square_loads = {}
    for number, block in enumerate((3, 2, 4, 1, 5, 0, 6)):
        part = pl.ds(block * PANEL, PANEL)
        square_loads[block] = pltpu.make_async_copy(p2.at[:, part], s.at[:, part], load_sem.at[8 + number])
    for load in loads:
        load.start()
    for block in (3, 2, 4, 1, 5, 0, 6):
        square_loads[block].start()

    loads[1].wait()
    pattern = pv[...].astype(F32).astype(BF16)
    position = lax.broadcasted_iota(jnp.int32, (BR, W), 1)
    slot = lax.broadcasted_iota(jnp.int32, (BR, W), 0)
    chosen = jnp.where(position == slot * CLASSES + c, 1.0, 0.0).astype(BF16)
    by_slot = dot_nt(chosen, pattern)
    block_row = lax.broadcasted_iota(jnp.int32, (BR, PANEL), 0)
    row_block = lax.broadcasted_iota(jnp.int32, (BR, PANEL), 1) // BS
    widen = jnp.where(block_row == row_block, 1.0, 0.0).astype(BF16)
    mask_rows[...] = jnp.dot(by_slot.astype(BF16), widen, preferred_element_type=F32)

    loads[0].wait()
    for k in range(WC):
        part = pl.ds(k * BS, BS)
        keep = jnp.broadcast_to(mask_rows[k : k + 1, :], (BS, PANEL)).astype(BF16)
        own[part, :] = dv[part, :] * keep

    pl.semaphore_wait(barrier, len(friends))

    def send(source, landing, sem, number, place):
        return pltpu.make_async_remote_copy(
            src_ref=source,
            dst_ref=landing,
            send_sem=send_sem.at[number],
            recv_sem=sem,
            device_id=place,
            device_id_type=MESH,
        )

    sides = {
        "even": (UP, up_in, up_sem, 1),
        "odd": (DOWN, down_in, down_sem, -1),
    }

    def landing(kind, d, chunk):
        first, count = chunk
        start = BASE[d] + first - (d * BS if kind == "even" else 0)
        return sides[kind][1].at[pl.ds(start, count)]

    def sends(kind):
        chunks, _, sem, sign = sides[kind]
        other = "odd" if kind == "even" else "even"
        other_chunks, _, other_sem, _ = sides[other]
        found = []
        for j in range(3):
            one, two = FIRST[1] + j, FIRST[2] + j
            far, near, back = chunks[2][j], chunks[1][j], other_chunks[1][j]
            found.append(send(own.at[pl.ds(*far)], landing(kind, 2, far), sem.at[two], 3 + j, at(2 * sign, 0)))
            found.append(send(own.at[pl.ds(*back)], landing(other, 1, back), other_sem.at[one], 6 + j, at(-sign, 0)))
            found.append(send(own.at[pl.ds(*near)], landing(kind, 1, near), sem.at[one], j, at(sign, 0)))
        return found

    @pl.when(even)
    def _():
        for copy in sends("even"):
            copy.start()

    @pl.when(odd)
    def _():
        for copy in sends("odd"):
            copy.start()

    def relays(kind, d, j):
        chunks, _, sem, sign = sides[kind]
        found = []

        def relay(to, number, place):
            chunk = chunks[to][j]
            found.append(
                send(landing(kind, d, chunk), landing(kind, to, chunk), sem.at[FIRST[to] + j], number, place)
            )

        if d == 1:
            if j < 2:
                relay(3, 9 + j, at(2 * sign, 0))
            relay(2, 11 + j, at(sign, 0))
        if d == 2 and j < 2:
            relay(3, 14 + j, at(sign, 0))
        return found

    def arrived(kind, d, j):
        chunks, _, sem, _ = sides[kind]
        place = landing(kind, d, chunks[d][j])
        send(place, place, sem.at[FIRST[d] + j], 0, at(-1, 0)).wait_recv()
        if d < 3:
            @pl.when(even if kind == "even" else odd)
            def _():
                for copy in relays(kind, d, j):
                    copy.start()

    position = lax.broadcasted_iota(jnp.int32, (W, PANEL), 0)
    natural = lax.broadcasted_iota(jnp.int32, (W, PANEL), 1) // BS
    for block in (3, 2, 4, 1, 5, 0, 6):
        square_loads[block].wait()
        chosen = jnp.where(position == natural + block * BR, 1.0, 0.0).astype(BF16)
        mask = jnp.dot(pattern, chosen, preferred_element_type=F32)
        for i in range(BR):
            keep = jnp.broadcast_to(mask[i : i + 1, :], (BS, PANEL)).astype(BF16)
            part = pl.ds(i * BS, BS)
            s[part, pl.ds(block * PANEL, PANEL)] = s[part, pl.ds(block * PANEL, PANEL)] * keep

    parity = lax.rem(c, 2)
    to_row = lax.broadcasted_iota(jnp.int32, (BS, TILE), 0)
    from_lane = lax.broadcasted_iota(jnp.int32, (BS, TILE), 1)
    pick = jnp.where(from_lane == to_row + parity * BS, -1.5, 0.0).astype(BF16)
    acc[...] = dot_nt(own[...], s[:, pl.ds(3 * PANEL, PANEL)])
    for k in range(WC):
        start = pl.multiple_of(k * PANEL + (c // 2) * TILE, TILE)
        part = pl.ds(k * BS, BS)
        acc[part, :] = acc[part, :] + dot_nt(pick, s[:, pl.ds(start, TILE)])

    def gather(kind, d, j):
        first, count = sides[kind][0][d][j]
        block = 3 - d if kind == "even" else 3 + d
        part = pl.ds(first - d * BS if kind == "even" else first + d * BS, count)
        place = landing(kind, d, (first, count))
        acc[part, :] = acc[part, :] + dot_nt(place[...], s[:, pl.ds(block * PANEL, PANEL)])

    for load in loads[2:]:
        load.wait()
    step_ids = lax.broadcasted_iota(jnp.int32, (2 * TILE, 32), 1)
    row_ids = lax.broadcasted_iota(jnp.int32, (2 * TILE, 32), 0)
    cell_ids = jnp.where(
        row_ids < CELLS - MARGIN, row_ids + MARGIN, jnp.where(row_ids < CELLS, row_ids - (CELLS - MARGIN), -1)
    )
    low = lax.broadcasted_iota(jnp.int32, (2 * TILE, TILE), 1) < BS

    def spread(values, offset, extent):
        hit = (cell_ids == offset + step_ids) & (step_ids < extent)
        onehot = jnp.where(hit, 1.0, 0.0).astype(BF16)
        return jnp.dot(onehot, values, preferred_element_type=F32)

    for t in range(4):
        part = pl.ds(t * TILE, TILE)
        pair = [spread(xbv[:, part], xov[2 * t + h], xev[2 * t + h]) for h in range(2)]
        spread_x[:, part] = jnp.where(low, pair[0], pair[1])[:CELLS].astype(BF16)
        if t < 3:
            pair = [spread(ybv[:, part], yov[0, 2 * t + h], yev[0, 2 * t + h]) for h in range(2)]
            spread_y[:, part] = jnp.where(low, pair[0], pair[1]).astype(BF16)
        else:
            part = pl.ds(t * TILE, BS)
            spread_y[:, part] = spread(ybv[:, part], yov[0, 6], yev[0, 6]).astype(BF16)

    for j in range(3):
        for d in (1, 2):
            for kind in ("even", "odd"):
                arrived(kind, d, j)
                gather(kind, d, j)
    for j in range(2):
        for kind in ("even", "odd"):
            arrived(kind, 3, j)
            gather(kind, 3, j)

    for k in range(WC):
        part = pl.ds(k * BS, BS)
        keep = jnp.broadcast_to(mask_rows[k : k + 1, :] * -2.0, (BS, PANEL))
        out_new[part, :] = (acc[part, :] * keep).astype(BF16)
    half_done = jnp.dot(spread_y[...], out_new[...], preferred_element_type=F32).astype(BF16)
    ext[...] = dot_nt(spread_x[...], half_done)

    def rim(number, source, place):
        return pltpu.make_async_remote_copy(
            src_ref=source,
            dst_ref=halo.at[number],
            send_sem=hsend_sem.at[number],
            recv_sem=halo_sem.at[number],
            device_id=place,
            device_id_type=MESH,
        )

    high_rows, low_rows = pl.ds(SX, MARGIN), pl.ds(SX + MARGIN, MARGIN)
    rims = [
        rim(4, ext.at[high_rows, pl.ds(TILE, TILE)], at(1, 1)),
        rim(5, ext.at[high_rows, pl.ds(TILE, TILE)], at(1, -1)),
        rim(6, ext.at[low_rows, pl.ds(TILE, TILE)], at(-1, 1)),
        rim(7, ext.at[low_rows, pl.ds(TILE, TILE)], at(-1, -1)),
        rim(0, ext.at[high_rows, pl.ds(0, TILE)], at(1, 0)),
        rim(1, ext.at[low_rows, pl.ds(0, TILE)], at(-1, 0)),
    ]
    for copy in rims:
        copy.start()
    lane = lax.broadcasted_iota(jnp.int32, (MARGIN, TILE), 1)
    group = lane // MARGIN
    margins = [jnp.zeros((MARGIN, TILE), F32), jnp.zeros((MARGIN, TILE), F32)]
    for g in range(4):
        piece = ext[g * MARGIN : (g + 1) * MARGIN, TILE : 2 * TILE]
        for side in range(2):
            turn = (MARGIN * (g - side)) % TILE
            turned = pltpu.roll(piece, turn, 1) if turn else piece
            margins[side] = jnp.where(group == g, turned, margins[side])
    packed[0] = margins[0]
    packed[1] = margins[1]
    late = [rim(2, packed.at[0], at(0, 1)), rim(3, packed.at[1], at(0, -1))]
    for copy in late:
        copy.start()

    for number in (0, 1, 2, 3, 4, 5, 6, 7):
        rim(number, halo.at[number], at(1, 0)).wait_recv()
    first, last = group == 0, group == 3
    for g in range(4):
        value = ext[g * MARGIN : (g + 1) * MARGIN, :TILE]
        turn = (-MARGIN * g) % TILE
        value = value + jnp.where(first, pltpu.roll(halo[2], turn, 1) if turn else halo[2], 0.0)
        turn = (MARGIN * (3 - g)) % TILE
        value = value + jnp.where(last, pltpu.roll(halo[3], turn, 1) if turn else halo[3], 0.0)
        if g == 0:
            value = value + halo[0]
            value = value + jnp.where(first, halo[4], 0.0) + jnp.where(last, pltpu.roll(halo[5], BS, 1), 0.0)
        if g == 3:
            value = value + halo[1]
            value = value + jnp.where(first, halo[6], 0.0) + jnp.where(last, pltpu.roll(halo[7], BS, 1), 0.0)
        out_grid[g * MARGIN : (g + 1) * MARGIN, :] = value

    @pl.when(even)
    def _():
        for copy in sends("even"):
            copy.wait_send()
        for d, j in ((1, 0), (1, 1), (1, 2), (2, 0), (2, 1)):
            for copy in relays("even", d, j):
                copy.wait_send()

    @pl.when(odd)
    def _():
        for copy in sends("odd"):
            copy.wait_send()
        for d, j in ((1, 0), (1, 1), (1, 2), (2, 0), (2, 1)):
            for copy in relays("odd", d, j):
                copy.wait_send()

    for copy in rims + late:
        copy.wait_send()


def solution(mesh):
    rows, cols = mesh.shape["row"], mesh.shape["col"]

    def shards(p2_panel, density, pattern, x_basis, x_offset, x_extent, y_basis, y_offset, y_extent):
        outside = pl.BlockSpec(memory_space=pltpu.HBM)
        inside = pl.BlockSpec(memory_space=pltpu.VMEM)
        new, grid = pl.pallas_call(
            functools.partial(kernel, rows, cols),
            out_shape=(
                jax.ShapeDtypeStruct((WC * BS, PANEL), BF16),
                jax.ShapeDtypeStruct((SX, TILE), F32),
            ),
            in_specs=[outside] * 9,
            out_specs=(inside, inside),
            scratch_shapes=[
                pltpu.VMEM((PANEL, W * BS), BF16),
                pltpu.VMEM((WC * BS, PANEL), BF16),
                pltpu.VMEM((BR, W), jnp.int32),
                pltpu.VMEM((32, PANEL), BF16),
                pltpu.VMEM((32, WC * BS), BF16),
                pltpu.SMEM((BR,), jnp.int32),
                pltpu.SMEM((BR,), jnp.int32),
                pltpu.SMEM((1, WC), jnp.int32),
                pltpu.SMEM((1, WC), jnp.int32),
                pltpu.VMEM((WC * BS, PANEL), BF16),
                pltpu.VMEM((IN_ROWS, PANEL), BF16),
                pltpu.VMEM((IN_ROWS, PANEL), BF16),
                pltpu.VMEM((WC * BS, PANEL), F32),
                pltpu.VMEM((CELLS, PANEL), BF16),
                pltpu.VMEM((2 * TILE, WC * BS), BF16),
                pltpu.VMEM((BR, PANEL), F32),
                pltpu.VMEM((CELLS, 2 * TILE), F32),
                pltpu.VMEM((2, MARGIN, TILE), F32),
                pltpu.VMEM((8, MARGIN, TILE), F32),
                pltpu.SemaphoreType.DMA((15,)),
                pltpu.SemaphoreType.DMA((16,)),
                pltpu.SemaphoreType.DMA((8,)),
                pltpu.SemaphoreType.DMA((8,)),
                pltpu.SemaphoreType.DMA((8,)),
                pltpu.SemaphoreType.DMA((8,)),
            ],
            compiler_params=pltpu.CompilerParams(
                collective_id=0, has_side_effects=True, vmem_limit_bytes=60 * 1024 * 1024
            ),
        )(
            p2_panel, density.T, pattern, x_basis.T, x_offset, x_extent, y_basis[0].T, y_offset, y_extent
        )
        return new.T, grid

    placed = (
        P("row", None),
        P("row", "col"),
        P("row", None),
        P("row", None),
        P("row"),
        P("row"),
        P("row", "col", None),
        P("row", "col"),
        P("row", "col"),
    )
    return jax.shard_map(
        shards,
        mesh=mesh,
        in_specs=placed,
        out_specs=(P("row", "col"), P("row", "col")),
        check_vma=False,
    )
```

time: 113 us -> 46 us (0.41)
  the two profiles are of different devices: /device:TPU:8 before, /device:TPU:1 now
where the time goes in v1:
time: 46 us; the launch traced here: 45.7 us
  Pallas kernels  41.8 us (91%)
  local copies, waits for them, and re-layouts  3.29 us (7%)
  between operations  0.64 us (1%)
    pallas_call x1, Pallas kernels, shards(): pl.pallas_call(functools.partial(kernel, rows, cols), out_shape=(jax.Shap...  41.8 us
    unnamed x2, local copies, waits for them, and re-layouts  3.29 us

profile of v1, /device:TPU:1, one launch (start us, length us, event | category | flops | bytes accessed | tf_op | source)
XLA Modules:
  0.0 45.7 jit_solution(2056761265653697276)
XLA Ops:
  0.6 41.8 %shard_map.104 = (bf16[448,512]{1,0:T(8,128)(2,1)}, f32[128,128]{1,0:T(8,128)}) custom-call(bf16[512,3584]{1,0:T(8,128)(2,1)} %p2.1, bf16[448,512]{1,0:T(8,128)(2,1)} %bitcast.6, s32[8,56]{1,0:T(8,128)} %pat.1, bf16[32,512]{1,0:T(8,128)(2,1)} %bitcast.8, s32[8]{0:T(128)} %xo.1, s32[8]{0:T(128)} %xe.1, bf16[32,448]{1,0:T(8,128)(2,1)} %bitcast.9, s32[1,7]{1,0:T(1,128)} %yo.1, ...), custom_call_target="tpu_custom_call" | custom-call | tf_op jit(solution)/shard_map/pallas_call | solution.py:317
  42.5 1.8 %copy.13 = bf16[512,448]{0,1:T(8,128)(2,1)} copy(bf16[512,448]{0,1:T(8,128)(2,1)} %bitcast.7) | data formatting | bytes 917504
  44.3 1.5 %copy.14 = f32[128,128]{1,0:T(8,128)} copy(f32[128,128]{1,0:T(8,128)} %get-tuple-element.9) | data formatting | bytes 131072

commit v2 on v1

--- a/solution.py
+++ b/solution.py
@@ -233,7 +233,7 @@
         keep = jnp.broadcast_to(mask_rows[k : k + 1, :] * -2.0, (BS, PANEL))
         out_new[part, :] = (acc[part, :] * keep).astype(BF16)
     half_done = jnp.dot(spread_y[...], out_new[...], preferred_element_type=F32).astype(BF16)
-    ext[...] = dot_nt(spread_x[...], half_done)
+    ext[SX:, :] = dot_nt(spread_x[SX:, :], half_done)
 
     def rim(number, source, place):
         return pltpu.make_async_remote_copy(
@@ -256,6 +256,7 @@
     ]
     for copy in rims:
         copy.start()
+    ext[:SX, :] = dot_nt(spread_x[:SX, :], half_done)
     lane = lax.broadcasted_iota(jnp.int32, (MARGIN, TILE), 1)
     group = lane // MARGIN
     margins = [jnp.zeros((MARGIN, TILE), F32), jnp.zeros((MARGIN, TILE), F32)]
@@ -308,6 +309,14 @@
         copy.wait_send()
 
 
+def finish(new, grid, out_new, out_grid, sem):
+    copies = [pltpu.make_async_copy(new, out_new, sem.at[0]), pltpu.make_async_copy(grid, out_grid, sem.at[1])]
+    for copy in copies:
+        copy.start()
+    for copy in copies:
+        copy.wait()
+
+
 def solution(mesh):
     rows, cols = mesh.shape["row"], mesh.shape["col"]
 
@@ -316,10 +325,7 @@
         inside = pl.BlockSpec(memory_space=pltpu.VMEM)
         new, grid = pl.pallas_call(
             functools.partial(kernel, rows, cols),
-            out_shape=(
-                jax.ShapeDtypeStruct((WC * BS, PANEL), BF16),
-                jax.ShapeDtypeStruct((SX, TILE), F32),
-            ),
+            out_shape=(pltpu.VMEM((WC * BS, PANEL), BF16), pltpu.VMEM((SX, TILE), F32)),
             in_specs=[outside] * 9,
             out_specs=(inside, inside),
             scratch_shapes=[
@@ -350,11 +356,22 @@
                 pltpu.SemaphoreType.DMA((8,)),
             ],
             compiler_params=pltpu.CompilerParams(
-                collective_id=0, has_side_effects=True, vmem_limit_bytes=60 * 1024 * 1024
+                collective_id=0, has_side_effects=True, vmem_limit_bytes=62914560
             ),
         )(
             p2_panel, density.T, pattern, x_basis.T, x_offset, x_extent, y_basis[0].T, y_offset, y_extent
         )
+        new, grid = pl.pallas_call(
+            finish,
+            out_shape=(
+                jax.ShapeDtypeStruct((WC * BS, PANEL), BF16),
+                jax.ShapeDtypeStruct((SX, TILE), F32),
+            ),
+            in_specs=[inside, inside],
+            out_specs=(outside, outside),
+            scratch_shapes=[pltpu.SemaphoreType.DMA((2,))],
+            compiler_params=pltpu.CompilerParams(vmem_limit_bytes=4 * 1024 * 1024),
+        )(new, grid)
         return new.T, grid
 
     placed = (

time: 46 us -> 42.6 us (0.926)
  local copies, waits for them, and re-layouts: 3.29 us -> 0 us
    unnamed x2 -> x0, local copies, waits for them, and re-layouts: 3.29 us -> none
    pallas_call x1 -> x2, Pallas kernels: 41.8 us -> 41.8 us  [the longest x1 41 us: shards(): pl.pallas_call(functools.partial(kernel, rows, cols), out_shape=(pltpu.VM...]
where the time goes in v2:
time: 42.6 us; the launch traced here: 42.4 us
  Pallas kernels  41.8 us (98%)
  between operations  0.64 us (2%)
    pallas_call x1, Pallas kernels, shards(): pl.pallas_call(functools.partial(kernel, rows, cols), out_shape=(pltpu.VM...  41 us

profile of v2, /device:TPU:1, one launch (start us, length us, event | category | flops | bytes accessed | tf_op | source)
XLA Modules:
  0.0 42.4 jit_solution(1015933291841381253)
XLA Ops:
  0.6 41.0 %shard_map.104 = (bf16[448,512]{1,0:T(8,128)(2,1)S(1)}, f32[128,128]{1,0:T(8,128)S(1)}) custom-call(bf16[512,3584]{1,0:T(8,128)(2,1)} %p2.1, bf16[448,512]{1,0:T(8,128)(2,1)} %bitcast.6, s32[8,56]{1,0:T(8,128)} %pat.1, bf16[32,512]{1,0:T(8,128)(2,1)} %bitcast.7, s32[8]{0:T(128)} %xo.1, s32[8]{0:T(128)} %xe.1, bf16[32,448]{1,0:T(8,128)(2,1)} %bitcast.8, ...), custom_call_target="tpu_custom_call" | custom-call | tf_op jit(solution)/shard_map/pallas_call | solution.py:326
  41.6 0.8 %shard_map.105 = (bf16[448,512]{1,0:T(8,128)(2,1)}, f32[128,128]{1,0:T(8,128)}) custom-call(bf16[448,512]{1,0:T(8,128)(2,1)S(1)} %get-tuple-element.6.new, f32[128,128]{1,0:T(8,128)S(1)} %get-tuple-element.7.grid), custom_call_target="tpu_custom_call" | custom-call | tf_op jit(solution)/shard_map/pallas_call | solution.py:364

commit v3 on v2

--- a/solution.py
+++ b/solution.py
@@ -155,15 +155,13 @@
             relay(3, 14 + j, at(sign, 0))
         return found
 
-    def arrived(kind, d, j):
+    def arrived(mine, kind, d, j):
         chunks, _, sem, _ = sides[kind]
         place = landing(kind, d, chunks[d][j])
         send(place, place, sem.at[FIRST[d] + j], 0, at(-1, 0)).wait_recv()
-        if d < 3:
-            @pl.when(even if kind == "even" else odd)
-            def _():
-                for copy in relays(kind, d, j):
-                    copy.start()
+        if d < 3 and kind == mine:
+            for copy in relays(kind, d, j):
+                copy.start()
 
     position = lax.broadcasted_iota(jnp.int32, (W, PANEL), 0)
     natural = lax.broadcasted_iota(jnp.int32, (W, PANEL), 1) // BS
@@ -186,8 +184,10 @@
         part = pl.ds(k * BS, BS)
         acc[part, :] = acc[part, :] + dot_nt(pick, s[:, pl.ds(start, TILE)])
 
-    def gather(kind, d, j):
-        first, count = sides[kind][0][d][j]
+    def gather(kind, d, parts):
+        chunks = [sides[kind][0][d][j] for j in parts]
+        first = min(chunk[0] for chunk in chunks)
+        count = sum(chunk[1] for chunk in chunks)
         block = 3 - d if kind == "even" else 3 + d
         part = pl.ds(first - d * BS if kind == "even" else first + d * BS, count)
         place = landing(kind, d, (first, count))
@@ -218,15 +218,25 @@
             part = pl.ds(t * TILE, BS)
             spread_y[:, part] = spread(ybv[:, part], yov[0, 6], yev[0, 6]).astype(BF16)
 
-    for j in range(3):
-        for d in (1, 2):
-            for kind in ("even", "odd"):
-                arrived(kind, d, j)
-                gather(kind, d, j)
-    for j in range(2):
-        for kind in ("even", "odd"):
-            arrived(kind, 3, j)
-            gather(kind, 3, j)
+    def collect(mine):
+        theirs = "odd" if mine == "even" else "even"
+        steps = (
+            (theirs, 1, (0, 1, 2)), (mine, 1, (0,)), (mine, 2, (0,)), (mine, 1, (1,)), (mine, 2, (1,)),
+            (theirs, 2, (0, 1)), (theirs, 3, (0, 1)), (mine, 2, (2,)), (mine, 1, (2,)), (theirs, 2, (2,)),
+            (mine, 3, (0,)), (mine, 3, (1,)),
+        )
+        for kind, d, parts in steps:
+            for j in parts:
+                arrived(mine, kind, d, j)
+            gather(kind, d, parts)
+
+    @pl.when(even)
+    def _():
+        collect("even")
+
+    @pl.when(odd)
+    def _():
+        collect("odd")
 
     for k in range(WC):
         part = pl.ds(k * BS, BS)

time: 42.6 us -> 41.5 us (0.974)
  Pallas kernels: 41.8 us -> 40.7 us
    pallas_call x1, Pallas kernels: 41 us -> 39.9 us  [shards(): pl.pallas_call(functools.partial(kernel, rows, cols), out_shape=(pltpu.VM...]
where the time goes in v3:
time: 41.5 us; the launch traced here: 41.3 us
  Pallas kernels  40.7 us (98%)
  between operations  0.64 us (2%)
    pallas_call x1, Pallas kernels, shards(): pl.pallas_call(functools.partial(kernel, rows, cols), out_shape=(pltpu.VM...  39.9 us

profile of v3, /device:TPU:1, one launch (start us, length us, event | category | flops | bytes accessed | tf_op | source)
XLA Modules:
  0.0 41.3 jit_solution(13889049421730510350)
XLA Ops:
  0.6 39.9 %shard_map.104 = (bf16[448,512]{1,0:T(8,128)(2,1)S(1)}, f32[128,128]{1,0:T(8,128)S(1)}) custom-call(bf16[512,3584]{1,0:T(8,128)(2,1)} %p2.1, bf16[448,512]{1,0:T(8,128)(2,1)} %bitcast.6, s32[8,56]{1,0:T(8,128)} %pat.1, bf16[32,512]{1,0:T(8,128)(2,1)} %bitcast.7, s32[8]{0:T(128)} %xo.1, s32[8]{0:T(128)} %xe.1, bf16[32,448]{1,0:T(8,128)(2,1)} %bitcast.8, ...), custom_call_target="tpu_custom_call" | custom-call | tf_op jit(solution)/shard_map/pallas_call | solution.py:336
  40.5 0.8 %shard_map.105 = (bf16[448,512]{1,0:T(8,128)(2,1)}, f32[128,128]{1,0:T(8,128)}) custom-call(bf16[448,512]{1,0:T(8,128)(2,1)S(1)} %get-tuple-element.6.new, f32[128,128]{1,0:T(8,128)S(1)} %get-tuple-element.7.grid), custom_call_target="tpu_custom_call" | custom-call | tf_op jit(solution)/shard_map/pallas_call | solution.py:374

commit v4 on v3

--- a/solution.py
+++ b/solution.py
@@ -45,8 +45,8 @@
     p2, dens, pat, xb, xo, xe, yb, yo, ye,
     out_new, out_grid,
     s, dv, pv, xbv, ybv, xov, xev, yov, yev,
-    own, up_in, down_in, acc, spread_x, spread_y, mask_rows, ext, packed, halo,
-    load_sem, send_sem, up_sem, down_sem, hsend_sem, halo_sem,
+    own, up_in, down_in, acc, spread_x, spread_y, mask_rows, ext, packed, halo, corner_out, corner_in, half_part, half,
+    load_sem, send_sem, up_sem, down_sem, hsend_sem, halo_sem, ready_sem,
 ):
     r = lax.axis_index("row")
     c = lax.axis_index("col")
@@ -57,9 +57,18 @@
         return (lax.rem(r + (dr + rows), rows), lax.rem(c + (dc + cols), cols))
 
     barrier = pltpu.get_barrier_semaphore()
-    friends = [(-1, 0), (1, 0), (-2, 0), (2, 0), (0, -1), (0, 1), (-1, -1), (-1, 1), (1, -1), (1, 1)]
-    for dr, dc in friends:
+    along_row = [(-1, 0), (1, 0), (-2, 0), (2, 0)]
+    aside = [(0, -1), (0, 1), (-1, -1), (1, 1), (-1, 1), (1, -1)]
+    for dr, dc in along_row:
         pl.semaphore_signal(barrier, inc=1, device_id=at(dr, dc), device_id_type=MESH)
+    before = len(along_row)
+    for dr, dc in aside:
+        other = at(dr, dc)
+        before = before + jnp.where(other[1] < c, 1, 0)
+
+        @pl.when(other[1] > c)
+        def _():
+            pl.semaphore_signal(barrier, inc=1, device_id=other, device_id_type=MESH)
 
     loads = []
     for number, (source, target) in enumerate(
@@ -92,7 +101,7 @@
         keep = jnp.broadcast_to(mask_rows[k : k + 1, :], (BS, PANEL)).astype(BF16)
         own[part, :] = dv[part, :] * keep
 
-    pl.semaphore_wait(barrier, len(friends))
+    pl.semaphore_wait(barrier, before)
 
     def send(source, landing, sem, number, place):
         return pltpu.make_async_remote_copy(
@@ -137,6 +146,13 @@
         for copy in sends("odd"):
             copy.start()
 
+    for number, (dr, dc) in enumerate(aside):
+        other = at(dr, dc)
+
+        @pl.when(other[1] < c)
+        def _():
+            pl.semaphore_signal(ready_sem.at[number ^ 1], inc=1, device_id=other, device_id_type=MESH)
+
     def relays(kind, d, j):
         chunks, _, sem, sign = sides[kind]
         found = []
@@ -218,6 +234,14 @@
             part = pl.ds(t * TILE, BS)
             spread_y[:, part] = spread(ybv[:, part], yov[0, 6], yev[0, 6]).astype(BF16)
 
+    def finish_rows(first, count):
+        for k in range(first // BS, (first + count) // BS):
+            part = pl.ds(k * BS, BS)
+            keep = jnp.broadcast_to(mask_rows[k : k + 1, :] * -2.0, (BS, PANEL))
+            out_new[part, :] = (acc[part, :] * keep).astype(BF16)
+        part = pl.ds(first, count)
+        return jnp.dot(spread_y[:, part], out_new[part, :], preferred_element_type=F32)
+
     def collect(mine):
         theirs = "odd" if mine == "even" else "even"
         steps = (
@@ -225,10 +249,14 @@
             (theirs, 2, (0, 1)), (theirs, 3, (0, 1)), (mine, 2, (2,)), (mine, 1, (2,)), (theirs, 2, (2,)),
             (mine, 3, (0,)), (mine, 3, (1,)),
         )
-        for kind, d, parts in steps:
+        early, late = ((128, 320), (0, 128)) if mine == "even" else ((0, 256), (256, 192))
+        for number, (kind, d, parts) in enumerate(steps):
+            if number == len(steps) - 1:
+                half_part[...] = finish_rows(*early)
             for j in parts:
                 arrived(mine, kind, d, j)
             gather(kind, d, parts)
+        half[...] = (half_part[...] + finish_rows(*late)).astype(BF16)
 
     @pl.when(even)
     def _():
@@ -238,66 +266,73 @@
     def _():
         collect("odd")
 
-    for k in range(WC):
-        part = pl.ds(k * BS, BS)
-        keep = jnp.broadcast_to(mask_rows[k : k + 1, :] * -2.0, (BS, PANEL))
-        out_new[part, :] = (acc[part, :] * keep).astype(BF16)
-    half_done = jnp.dot(spread_y[...], out_new[...], preferred_element_type=F32).astype(BF16)
+    for number, (dr, dc) in enumerate(aside):
+        @pl.when(at(dr, dc)[1] > c)
+        def _():
+            pl.semaphore_wait(ready_sem.at[number], 1)
+
+    half_done = half[...]
     ext[SX:, :] = dot_nt(spread_x[SX:, :], half_done)
 
-    def rim(number, source, place):
+    def rim(number, source, place, box, slot):
         return pltpu.make_async_remote_copy(
             src_ref=source,
-            dst_ref=halo.at[number],
+            dst_ref=box.at[slot],
             send_sem=hsend_sem.at[number],
             recv_sem=halo_sem.at[number],
             device_id=place,
             device_id_type=MESH,
         )
 
-    high_rows, low_rows = pl.ds(SX, MARGIN), pl.ds(SX + MARGIN, MARGIN)
     rims = [
-        rim(4, ext.at[high_rows, pl.ds(TILE, TILE)], at(1, 1)),
-        rim(5, ext.at[high_rows, pl.ds(TILE, TILE)], at(1, -1)),
-        rim(6, ext.at[low_rows, pl.ds(TILE, TILE)], at(-1, 1)),
-        rim(7, ext.at[low_rows, pl.ds(TILE, TILE)], at(-1, -1)),
-        rim(0, ext.at[high_rows, pl.ds(0, TILE)], at(1, 0)),
-        rim(1, ext.at[low_rows, pl.ds(0, TILE)], at(-1, 0)),
+        rim(0, ext.at[pl.ds(SX, MARGIN), pl.ds(0, TILE)], at(1, 0), halo, 0),
+        rim(1, ext.at[pl.ds(SX + MARGIN, MARGIN), pl.ds(0, TILE)], at(-1, 0), halo, 1),
     ]
     for copy in rims:
         copy.start()
+
+    def pack(first_row, height, side):
+        group = lax.broadcasted_iota(jnp.int32, (height, TILE), 1) // MARGIN
+        joined = jnp.zeros((height, TILE), F32)
+        for g in range(4):
+            start = first_row + g * height
+            piece = ext[start : start + height, TILE : 2 * TILE]
+            turn = (MARGIN * (g - side)) % TILE
+            joined = jnp.where(group == g, pltpu.roll(piece, turn, 1) if turn else piece, joined)
+        return joined
+
+    def unpack(value, g, side):
+        turn = (MARGIN * (3 - g)) % TILE if side else (-MARGIN * g) % TILE
+        value = pltpu.roll(value, turn, 1) if turn else value
+        group = lax.broadcasted_iota(jnp.int32, value.shape, 1) // MARGIN
+        return jnp.where(group == (3 if side else 0), value, 0.0)
+
+    for number, (dr, dc) in enumerate(((1, 1), (1, -1), (-1, 1), (-1, -1))):
+        corner_out[number] = pack(SX if dr > 0 else SX + MARGIN, MARGIN // 4, 0 if dc > 0 else 1)
+        rims.append(rim(4 + number, corner_out.at[number], at(dr, dc), corner_in, number))
+        rims[-1].start()
     ext[:SX, :] = dot_nt(spread_x[:SX, :], half_done)
-    lane = lax.broadcasted_iota(jnp.int32, (MARGIN, TILE), 1)
-    group = lane // MARGIN
-    margins = [jnp.zeros((MARGIN, TILE), F32), jnp.zeros((MARGIN, TILE), F32)]
-    for g in range(4):
-        piece = ext[g * MARGIN : (g + 1) * MARGIN, TILE : 2 * TILE]
-        for side in range(2):
-            turn = (MARGIN * (g - side)) % TILE
-            turned = pltpu.roll(piece, turn, 1) if turn else piece
-            margins[side] = jnp.where(group == g, turned, margins[side])
-    packed[0] = margins[0]
-    packed[1] = margins[1]
-    late = [rim(2, packed.at[0], at(0, 1)), rim(3, packed.at[1], at(0, -1))]
-    for copy in late:
-        copy.start()
-
-    for number in (0, 1, 2, 3, 4, 5, 6, 7):
-        rim(number, halo.at[number], at(1, 0)).wait_recv()
-    first, last = group == 0, group == 3
+    for number, dc in enumerate((1, -1)):
+        packed[number] = pack(0, MARGIN, number)
+        rims.append(rim(2 + number, packed.at[number], at(0, dc), halo, 2 + number))
+        rims[-1].start()
+
+    for number in range(4):
+        rim(number, halo.at[number], at(1, 0), halo, number).wait_recv()
     for g in range(4):
         value = ext[g * MARGIN : (g + 1) * MARGIN, :TILE]
-        turn = (-MARGIN * g) % TILE
-        value = value + jnp.where(first, pltpu.roll(halo[2], turn, 1) if turn else halo[2], 0.0)
-        turn = (MARGIN * (3 - g)) % TILE
-        value = value + jnp.where(last, pltpu.roll(halo[3], turn, 1) if turn else halo[3], 0.0)
-        if g == 0:
-            value = value + halo[0]
-            value = value + jnp.where(first, halo[4], 0.0) + jnp.where(last, pltpu.roll(halo[5], BS, 1), 0.0)
-        if g == 3:
-            value = value + halo[1]
-            value = value + jnp.where(first, halo[6], 0.0) + jnp.where(last, pltpu.roll(halo[7], BS, 1), 0.0)
+        value = value + unpack(halo[2], g, 0) + unpack(halo[3], g, 1)
+        if g in (0, 3):
+            value = value + halo[0 if g == 0 else 1]
         out_grid[g * MARGIN : (g + 1) * MARGIN, :] = value
+    for number in range(4):
+        rim(4 + number, corner_in.at[number], at(1, 0), corner_in, number).wait_recv()
+    height = MARGIN // 4
+    for start, pair in ((0, (0, 1)), (SX - MARGIN, (2, 3))):
+        for g in range(4):
+            part = pl.ds(start + g * height, height)
+            rest = unpack(corner_in[pair[0]], g, 0) + unpack(corner_in[pair[1]], g, 1)
+            out_grid[part, :] = out_grid[part, :] + rest
 
     @pl.when(even)
     def _():
@@ -315,7 +350,7 @@
             for copy in relays("odd", d, j):
                 copy.wait_send()
 
-    for copy in rims + late:
+    for copy in rims:
         copy.wait_send()
 
 
@@ -357,13 +392,18 @@
                 pltpu.VMEM((BR, PANEL), F32),
                 pltpu.VMEM((CELLS, 2 * TILE), F32),
                 pltpu.VMEM((2, MARGIN, TILE), F32),
-                pltpu.VMEM((8, MARGIN, TILE), F32),
+                pltpu.VMEM((4, MARGIN, TILE), F32),
+                pltpu.VMEM((4, MARGIN // 4, TILE), F32),
+                pltpu.VMEM((4, MARGIN // 4, TILE), F32),
+                pltpu.VMEM((2 * TILE, PANEL), F32),
+                pltpu.VMEM((2 * TILE, PANEL), BF16),
                 pltpu.SemaphoreType.DMA((15,)),
                 pltpu.SemaphoreType.DMA((16,)),
                 pltpu.SemaphoreType.DMA((8,)),
                 pltpu.SemaphoreType.DMA((8,)),
                 pltpu.SemaphoreType.DMA((8,)),
                 pltpu.SemaphoreType.DMA((8,)),
+                pltpu.SemaphoreType.REGULAR((6,)),
             ],
             compiler_params=pltpu.CompilerParams(
                 collective_id=0, has_side_effects=True, vmem_limit_bytes=62914560

time: 41.5 us -> 41.2 us (level)
  no operation moved by 1% of the time
where the time goes in v4:
time: 41.2 us; the launch traced here: 41 us
  Pallas kernels  40.3 us (98%)
  between operations  0.64 us (2%)
    pallas_call x1, Pallas kernels, shards(): pl.pallas_call(functools.partial(kernel, rows, cols), out_shape=(pltpu.VM...  39.5 us

profile of v4, /device:TPU:1, one launch (start us, length us, event | category | flops | bytes accessed | tf_op | source)
XLA Modules:
  0.0 41.0 jit_solution(8655078681495423015)
XLA Ops:
  0.6 39.5 %shard_map.104 = (bf16[448,512]{1,0:T(8,128)(2,1)S(1)}, f32[128,128]{1,0:T(8,128)S(1)}) custom-call(bf16[512,3584]{1,0:T(8,128)(2,1)} %p2.1, bf16[448,512]{1,0:T(8,128)(2,1)} %bitcast.6, s32[8,56]{1,0:T(8,128)} %pat.1, bf16[32,512]{1,0:T(8,128)(2,1)} %bitcast.7, s32[8]{0:T(128)} %xo.1, s32[8]{0:T(128)} %xe.1, bf16[32,448]{1,0:T(8,128)(2,1)} %bitcast.8, ...), custom_call_target="tpu_custom_call" | custom-call | tf_op jit(solution)/shard_map/pallas_call | solution.py:371
  40.2 0.8 %shard_map.105 = (bf16[448,512]{1,0:T(8,128)(2,1)}, f32[128,128]{1,0:T(8,128)}) custom-call(bf16[448,512]{1,0:T(8,128)(2,1)S(1)} %get-tuple-element.6.new, f32[128,128]{1,0:T(8,128)S(1)} %get-tuple-element.7.grid), custom_call_target="tpu_custom_call" | custom-call | tf_op jit(solution)/shard_map/pallas_call | solution.py:414

commit v5 on v4

--- a/solution.py
+++ b/solution.py
@@ -272,7 +272,8 @@
             pl.semaphore_wait(ready_sem.at[number], 1)
 
     half_done = half[...]
-    ext[SX:, :] = dot_nt(spread_x[SX:, :], half_done)
+    ext[SX:, :TILE] = dot_nt(spread_x[SX:, :], half_done[:TILE])
+    ext[:, TILE:] = dot_nt(spread_x[...], half_done[TILE:])
 
     def rim(number, source, place, box, slot):
         return pltpu.make_async_remote_copy(
@@ -311,11 +312,11 @@
         corner_out[number] = pack(SX if dr > 0 else SX + MARGIN, MARGIN // 4, 0 if dc > 0 else 1)
         rims.append(rim(4 + number, corner_out.at[number], at(dr, dc), corner_in, number))
         rims[-1].start()
-    ext[:SX, :] = dot_nt(spread_x[:SX, :], half_done)
     for number, dc in enumerate((1, -1)):
         packed[number] = pack(0, MARGIN, number)
         rims.append(rim(2 + number, packed.at[number], at(0, dc), halo, 2 + number))
         rims[-1].start()
+    ext[:SX, :TILE] = dot_nt(spread_x[:SX, :], half_done[:TILE])
 
     for number in range(4):
         rim(number, halo.at[number], at(1, 0), halo, number).wait_recv()

time: 41.2 us -> 41.2 us (level)
  no operation moved by 1% of the time
where the time goes in v5:
time: 41.2 us; the launch traced here: 41 us
  Pallas kernels  40.3 us (98%)
  between operations  0.64 us (2%)
    pallas_call x1, Pallas kernels, shards(): pl.pallas_call(functools.partial(kernel, rows, cols), out_shape=(pltpu.VM...  39.5 us

profile of v5, /device:TPU:1, one launch (start us, length us, event | category | flops | bytes accessed | tf_op | source)
XLA Modules:
  0.0 41.0 jit_solution(5368360212516394271)
XLA Ops:
  0.6 39.5 %shard_map.104 = (bf16[448,512]{1,0:T(8,128)(2,1)S(1)}, f32[128,128]{1,0:T(8,128)S(1)}) custom-call(bf16[512,3584]{1,0:T(8,128)(2,1)} %p2.1, bf16[448,512]{1,0:T(8,128)(2,1)} %bitcast.6, s32[8,56]{1,0:T(8,128)} %pat.1, bf16[32,512]{1,0:T(8,128)(2,1)} %bitcast.7, s32[8]{0:T(128)} %xo.1, s32[8]{0:T(128)} %xe.1, bf16[32,448]{1,0:T(8,128)(2,1)} %bitcast.8, ...), custom_call_target="tpu_custom_call" | custom-call | tf_op jit(solution)/shard_map/pallas_call | solution.py:372
  40.2 0.8 %shard_map.105 = (bf16[448,512]{1,0:T(8,128)(2,1)}, f32[128,128]{1,0:T(8,128)}) custom-call(bf16[448,512]{1,0:T(8,128)(2,1)S(1)} %get-tuple-element.6.new, f32[128,128]{1,0:T(8,128)S(1)} %get-tuple-element.7.grid), custom_call_target="tpu_custom_call" | custom-call | tf_op jit(solution)/shard_map/pallas_call | solution.py:415

commit v6 on v5

--- a/solution.py
+++ b/solution.py
@@ -285,10 +285,10 @@
             device_id_type=MESH,
         )
 
-    rims = [
-        rim(0, ext.at[pl.ds(SX, MARGIN), pl.ds(0, TILE)], at(1, 0), halo, 0),
-        rim(1, ext.at[pl.ds(SX + MARGIN, MARGIN), pl.ds(0, TILE)], at(-1, 0), halo, 1),
-    ]
+    for number in range(2):
+        start = SX + number * MARGIN
+        packed[number] = ext[start : start + MARGIN, :TILE].astype(BF16)
+    rims = [rim(0, packed.at[0], at(1, 0), halo, 0), rim(1, packed.at[1], at(-1, 0), halo, 1)]
     for copy in rims:
         copy.start()
 
@@ -313,18 +313,19 @@
         rims.append(rim(4 + number, corner_out.at[number], at(dr, dc), corner_in, number))
         rims[-1].start()
     for number, dc in enumerate((1, -1)):
-        packed[number] = pack(0, MARGIN, number)
-        rims.append(rim(2 + number, packed.at[number], at(0, dc), halo, 2 + number))
+        packed[2 + number] = pack(0, MARGIN, number).astype(BF16)
+        rims.append(rim(2 + number, packed.at[2 + number], at(0, dc), halo, 2 + number))
         rims[-1].start()
     ext[:SX, :TILE] = dot_nt(spread_x[:SX, :], half_done[:TILE])
 
     for number in range(4):
         rim(number, halo.at[number], at(1, 0), halo, number).wait_recv()
+    aside_low, aside_high = halo[2].astype(F32), halo[3].astype(F32)
     for g in range(4):
         value = ext[g * MARGIN : (g + 1) * MARGIN, :TILE]
-        value = value + unpack(halo[2], g, 0) + unpack(halo[3], g, 1)
+        value = value + unpack(aside_low, g, 0) + unpack(aside_high, g, 1)
         if g in (0, 3):
-            value = value + halo[0 if g == 0 else 1]
+            value = value + halo[0 if g == 0 else 1].astype(F32)
         out_grid[g * MARGIN : (g + 1) * MARGIN, :] = value
     for number in range(4):
         rim(4 + number, corner_in.at[number], at(1, 0), corner_in, number).wait_recv()
@@ -392,8 +393,8 @@
                 pltpu.VMEM((2 * TILE, WC * BS), BF16),
                 pltpu.VMEM((BR, PANEL), F32),
                 pltpu.VMEM((CELLS, 2 * TILE), F32),
-                pltpu.VMEM((2, MARGIN, TILE), F32),
-                pltpu.VMEM((4, MARGIN, TILE), F32),
+                pltpu.VMEM((4, MARGIN, TILE), BF16),
+                pltpu.VMEM((4, MARGIN, TILE), BF16),
                 pltpu.VMEM((4, MARGIN // 4, TILE), F32),
                 pltpu.VMEM((4, MARGIN // 4, TILE), F32),
                 pltpu.VMEM((2 * TILE, PANEL), F32),

time: 41.2 us -> 41.1 us (level)
  no operation moved by 1% of the time
where the time goes in v6:
time: 41.1 us; the launch traced here: 41 us
  Pallas kernels  40.3 us (98%)
  between operations  0.64 us (2%)
    pallas_call x1, Pallas kernels, shards(): pl.pallas_call(functools.partial(kernel, rows, cols), out_shape=(pltpu.VM...  39.5 us

profile of v6, /device:TPU:1, one launch (start us, length us, event | category | flops | bytes accessed | tf_op | source)
XLA Modules:
  0.0 41.0 jit_solution(8823931953099264703)
XLA Ops:
  0.6 39.5 %shard_map.104 = (bf16[448,512]{1,0:T(8,128)(2,1)S(1)}, f32[128,128]{1,0:T(8,128)S(1)}) custom-call(bf16[512,3584]{1,0:T(8,128)(2,1)} %p2.1, bf16[448,512]{1,0:T(8,128)(2,1)} %bitcast.6, s32[8,56]{1,0:T(8,128)} %pat.1, bf16[32,512]{1,0:T(8,128)(2,1)} %bitcast.7, s32[8]{0:T(128)} %xo.1, s32[8]{0:T(128)} %xe.1, bf16[32,448]{1,0:T(8,128)(2,1)} %bitcast.8, ...), custom_call_target="tpu_custom_call" | custom-call | tf_op jit(solution)/shard_map/pallas_call | solution.py:373
  40.2 0.8 %shard_map.105 = (bf16[448,512]{1,0:T(8,128)(2,1)}, f32[128,128]{1,0:T(8,128)}) custom-call(bf16[448,512]{1,0:T(8,128)(2,1)S(1)} %get-tuple-element.6.new, f32[128,128]{1,0:T(8,128)S(1)} %get-tuple-element.7.grid), custom_call_target="tpu_custom_call" | custom-call | tf_op jit(solution)/shard_map/pallas_call | solution.py:416
